TPU v7x, 32 devices: a whole 2x2x4 slice. The times are simulated.
32 devices in a mesh: ctx: 8 (over y, x, core), fsdp: 4 (over z).
Axes of the slice: x: 2, y: 2, z: 4, core: 2. Of those that a mesh axis runs over, the one named last changes fastest.
Arguments:
- tokens: bfloat16 [4, 2048, 2048], P('fsdp', 'ctx'), may hold values from -6 to 6
- cotangent: bfloat16 [4, 2048, 2048], P('fsdp', 'ctx'), may hold values from -6 to 6
- doc_starts: int32 [4, 8], P('fsdp'), may hold values from 0 to 2047, as said below
- deal_order: int32 [16], replicated, may hold values from 0 to 15, as said below
- query_key_value_weight: bfloat16 [2048, 1536], P('fsdp'), may hold values from -0.125 to 0.125
- w_out: bfloat16 [1024, 2048], P('fsdp'), may hold values from -1.5 to 1.5
- w_gate: bfloat16 [2048, 1024], P('fsdp'), may hold values from -0.125 to 0.125
- w_up: bfloat16 [2048, 1024], P('fsdp'), may hold values from -0.125 to 0.125
- w_down: bfloat16 [1024, 2048], P('fsdp'), may hold values from -0.1875 to 0.1875
- gain_attn: bfloat16 [2048], P('fsdp'), may hold values from 0.5 to 1.5
- gain_ffn: bfloat16 [2048], P('fsdp'), may hold values from 0.5 to 1.5
- gain_qk: bfloat16 [2, 64], P(None, 'fsdp'), may hold values from 1 to 2
Outputs:
- mixed_out: bfloat16 [4, 2048, 2048], P('fsdp', 'ctx')
- tokens_grad: float32 [4, 2048, 2048], P('fsdp', 'ctx')
- w_qkv_grad: float32 [2048, 1536], P('fsdp')
- w_out_grad: float32 [1024, 2048], P('fsdp')
- w_gate_grad: float32 [2048, 1024], P('fsdp')
- w_up_grad: float32 [2048, 1024], P('fsdp')
- w_down_grad: float32 [1024, 2048], P('fsdp')
- gain_attn_grad: float32 [2048], P('fsdp')
- gain_ffn_grad: float32 [2048], P('fsdp')
- gain_qk_grad: float32 [2, 64], P(None, 'fsdp')
Inputs may be any that keep to these rules, and one draw needn't show every extreme that they name: `doc_starts`: in each pack the first entry is 0 and entries rise; every document (from its start to the next start, the last one to 2048) holds 1 to 1024 tokens, one document of each pack holds exactly 1024, and the last document of each pack holds one token, so its start is 2047. `deal_order`: A permutation of the 16 blocks of a pack; the blocks at stored places 2 c and 2 c + 1 add up to 15.
All inputs are finite; a program needn't handle non-finite values.
Results may differ from a plain program's by a relative error of at most 0.017.
The roundings to bfloat16 on the way count: a program that leaves them out, or rounds other values in their place, can miss the bound.
Values may be sent and summed in bfloat16 or wider, within the bound.
A program may use at most 192 MiB of HBM per device.

v0:
```python
import math
import jax
import jax.numpy as jnp
from jax import lax
from jax.sharding import PartitionSpec as P

QUERY_HEADS = 16
KEY_VALUE_HEADS = 4
HEAD_SIZE = 64
EPSILON = 1e-06
THETA = 10000.0


def times_transposed(left, right):
    return lax.dot_general(
        left, right, (((1,), (1,)), ((), ())), preferred_element_type=jnp.float32
    )


def transposed_times(left, right):
    return lax.dot_general(
        left, right, (((0,), (0,)), ((), ())), preferred_element_type=jnp.float32
    )


def norm_forward(values, gain_vec):
    inverse = lax.rsqrt(jnp.mean(values * values, axis=-1, keepdims=True) + EPSILON)
    return (values * inverse * gain_vec, inverse)


def norm_backward(values, inverse, gain_vec, grad_out):
    scaled = grad_out * gain_vec
    grad_in = inverse * (
        scaled - values * inverse * inverse * jnp.mean(scaled * values, axis=-1, keepdims=True)
    )
    return (grad_in, grad_out * values * inverse)


def rotate(values, cosines, sine_vals):
    half_dim = values.shape[-1] // 2
    first_half = values[..., :half_dim]
    second_half = values[..., half_dim:]
    return jnp.concatenate(
        [
            first_half * cosines - second_half * sine_vals,
            second_half * cosines + first_half * sine_vals,
        ],
        axis=-1,
    )


def rotate_back(grad_out, cosines, sine_vals):
    half_dim = grad_out.shape[-1] // 2
    first_half = grad_out[..., :half_dim]
    second_half = grad_out[..., half_dim:]
    return jnp.concatenate(
        [
            first_half * cosines + second_half * sine_vals,
            second_half * cosines - first_half * sine_vals,
        ],
        axis=-1,
    )


def rotary_tables(position, doc_begin):
    offsets = (position - doc_begin).astype(jnp.float32)
    frequency = THETA ** (-jnp.arange(0, HEAD_SIZE // 2, dtype=jnp.float32) * 2.0 / HEAD_SIZE)
    angles = offsets[:, None] * frequency[None, :]
    return (jnp.cos(angles)[:, None, :], jnp.sin(angles)[:, None, :])


def per_device(
    tokens,
    cotangent,
    doc_starts,
    deal_order,
    query_key_value_weight,
    w_out,
    w_gate,
    w_up,
    w_down,
    gain_attn,
    gain_ffn,
    gain_qk,
):
    ctx_count = lax.axis_size("ctx")
    fsdp_count = lax.axis_size("fsdp")
    ctx_rank = lax.axis_index("ctx")
    qkv_full, out_full, attn_gathered, qk_gathered = (
        lax.all_gather(query_key_value_weight, "fsdp", axis=0, tiled=True),
        lax.all_gather(w_out, "fsdp", axis=0, tiled=True),
        lax.all_gather(gain_attn, "fsdp", axis=0, tiled=True),
        lax.all_gather(gain_qk, "fsdp", axis=1, tiled=True),
    )
    gate_full, up_full, down_full, ffn_gathered = (
        lax.all_gather(w_gate, "fsdp", axis=0, tiled=True),
        lax.all_gather(w_up, "fsdp", axis=0, tiled=True),
        lax.all_gather(w_down, "fsdp", axis=0, tiled=True),
        lax.all_gather(gain_ffn, "fsdp", axis=0, tiled=True),
    )
    attn_gain = attn_gathered.astype(jnp.float32)
    ffn_gain = ffn_gathered.astype(jnp.float32)
    query_gain = qk_gathered[0].astype(jnp.float32)
    key_gain = qk_gathered[1].astype(jnp.float32)
    pack_in = tokens[0].astype(jnp.float32)
    token_rows = pack_in.shape[0]
    block_len = token_rows // 2
    full_len = token_rows * ctx_count
    key_value_width = KEY_VALUE_HEADS * HEAD_SIZE
    group_width = QUERY_HEADS // KEY_VALUE_HEADS
    inv_root = HEAD_SIZE ** (-0.5)
    start_row = doc_starts[0]
    stored = jnp.arange(full_len, dtype=jnp.int32)
    key_place = (
        jnp.repeat(deal_order, block_len, total_repeat_length=full_len) * block_len
        + stored % block_len
    )
    key_begin = jnp.max(
        jnp.where(start_row[None, :] <= key_place[:, None], start_row[None, :], 0), axis=1
    )
    query_place = lax.dynamic_slice_in_dim(key_place, ctx_rank * token_rows, token_rows)
    query_begin = lax.dynamic_slice_in_dim(key_begin, ctx_rank * token_rows, token_rows)
    cosines, sine_vals = rotary_tables(query_place, query_begin)
    normed, attn_inverse = norm_forward(pack_in, attn_gain)
    normed_low = normed.astype(jnp.bfloat16)
    projected_rows = jnp.dot(normed_low, qkv_full, preferred_element_type=jnp.float32)
    query_raw = projected_rows[:, : QUERY_HEADS * HEAD_SIZE].reshape(
        token_rows, QUERY_HEADS, HEAD_SIZE
    )
    unrotated_key = projected_rows[
        :, QUERY_HEADS * HEAD_SIZE : (QUERY_HEADS + KEY_VALUE_HEADS) * HEAD_SIZE
    ].reshape(token_rows, KEY_VALUE_HEADS, HEAD_SIZE)
    unprojected_value = projected_rows[:, (QUERY_HEADS + KEY_VALUE_HEADS) * HEAD_SIZE :]
    query_normed, query_inverse = norm_forward(query_raw, query_gain)
    key_normed, key_inverse = norm_forward(unrotated_key, key_gain)
    query_heads_rows = rotate(query_normed, cosines, sine_vals).astype(jnp.bfloat16)
    key_local = rotate(key_normed, cosines, sine_vals).astype(jnp.bfloat16)
    local_pair = jnp.concatenate(
        [key_local.reshape(token_rows, key_value_width), unprojected_value.astype(jnp.bfloat16)],
        axis=1,
    )
    every_pair = lax.all_gather(local_pair, "ctx", axis=0, tiled=True)
    key_block_index = math.gcd(full_len, 512)
    block_total = full_len // key_block_index
    key_block_list = (
        every_pair[:, :key_value_width].reshape(
            block_total, key_block_index, KEY_VALUE_HEADS, HEAD_SIZE
        ),
        key_place.reshape(block_total, key_block_index),
        key_begin.reshape(block_total, key_block_index),
        every_pair[:, key_value_width:].reshape(
            block_total, key_block_index, KEY_VALUE_HEADS, HEAD_SIZE
        ),
    )
    grouped_heads = query_heads_rows.reshape(token_rows, KEY_VALUE_HEADS, group_width, HEAD_SIZE)

    def block_scores(key_tile, place_tile, begin_tile):
        raw_scores = (
            jnp.einsum(
                "qkgd,tkd->kgqt", grouped_heads, key_tile, preferred_element_type=jnp.float32
            )
            * inv_root
        )
        allowed = (query_begin[:, None] == begin_tile[None, :]) & (
            place_tile[None, :] <= query_place[:, None]
        )
        return jnp.where(allowed[None, None], raw_scores, -1e30)

    def stats_step(carry, tiles):
        row_max, row_sum = carry
        scores = block_scores(tiles[0], tiles[1], tiles[2])
        new_max = jnp.maximum(row_max, jnp.max(scores, axis=-1))
        row_sum = row_sum * jnp.exp(row_max - new_max) + jnp.sum(
            jnp.exp(scores - new_max[..., None]), axis=-1
        )
        return ((new_max, row_sum), None)

    initial_maximum = jnp.full((KEY_VALUE_HEADS, group_width, token_rows), -1e30, jnp.float32)
    initial_sum = jnp.zeros((KEY_VALUE_HEADS, group_width, token_rows), jnp.float32)
    (row_max, row_sum), unused = lax.scan(
        stats_step, (initial_maximum, initial_sum), key_block_list
    )

    def block_probs(tiles):
        scores = block_scores(tiles[0], tiles[1], tiles[2])
        return jnp.exp(scores - row_max[..., None]) / row_sum[..., None]

    def output_update(running, tiles):
        soft_probs = block_probs(tiles).astype(jnp.bfloat16)
        return (
            running
            + jnp.einsum(
                "kgqt,tkd->qkgd", soft_probs, tiles[3], preferred_element_type=jnp.float32
            ),
            None,
        )

    attended_sum, unused = lax.scan(
        output_update,
        jnp.zeros((token_rows, KEY_VALUE_HEADS, group_width, HEAD_SIZE), jnp.float32),
        key_block_list,
    )
    attended = attended_sum.reshape(token_rows, QUERY_HEADS * HEAD_SIZE).astype(jnp.bfloat16)
    hidden_in = pack_in + jnp.dot(attended, out_full, preferred_element_type=jnp.float32)
    normed_ffn, ffn_inverse = norm_forward(hidden_in, ffn_gain)
    normed_ffn_low = normed_ffn.astype(jnp.bfloat16)
    gate_act = jnp.dot(normed_ffn_low, gate_full, preferred_element_type=jnp.float32)
    upward = jnp.dot(normed_ffn_low, up_full, preferred_element_type=jnp.float32)
    sigmoid_gate = jax.nn.sigmoid(gate_act)
    hidden = (gate_act * sigmoid_gate * upward).astype(jnp.bfloat16)
    mixed_out = (hidden_in + jnp.dot(hidden, down_full, preferred_element_type=jnp.float32)).astype(
        jnp.bfloat16
    )
    grad_mixed = cotangent[0]
    grad_hidden = times_transposed(grad_mixed, down_full)
    grad_gate = (
        grad_hidden * upward * sigmoid_gate * (1.0 + gate_act * (1.0 - sigmoid_gate))
    ).astype(jnp.bfloat16)
    grad_up = (grad_hidden * gate_act * sigmoid_gate).astype(jnp.bfloat16)
    grad_normed_ffn = times_transposed(grad_gate, gate_full) + times_transposed(grad_up, up_full)
    grad_resid_part, ffn_gain_part = norm_backward(
        hidden_in, ffn_inverse, ffn_gain, grad_normed_ffn
    )
    grad_resid = grad_mixed.astype(jnp.float32) + grad_resid_part
    grad_branch = grad_resid.astype(jnp.bfloat16)
    attended_gradient = times_transposed(grad_branch, out_full).astype(jnp.bfloat16)
    grouped_gradient = attended_gradient.reshape(
        token_rows, KEY_VALUE_HEADS, group_width, HEAD_SIZE
    )

    def delta_update(running, tiles):
        soft_probs = block_probs(tiles)
        grad_probs = jnp.einsum(
            "qkgd,tkd->kgqt", grouped_gradient, tiles[3], preferred_element_type=jnp.float32
        )
        return (running + jnp.sum(soft_probs * grad_probs, axis=-1), None)

    row_delta, unused = lax.scan(
        delta_update,
        jnp.zeros((KEY_VALUE_HEADS, group_width, token_rows), jnp.float32),
        key_block_list,
    )

    def gradient_update(running, tiles):
        soft_probs = block_probs(tiles)
        grad_probs = jnp.einsum(
            "qkgd,tkd->kgqt", grouped_gradient, tiles[3], preferred_element_type=jnp.float32
        )
        grad_scores = (soft_probs * (grad_probs - row_delta[..., None])).astype(jnp.bfloat16)
        running = running + jnp.einsum(
            "kgqt,tkd->qkgd", grad_scores, tiles[0], preferred_element_type=jnp.float32
        )
        grad_keys = (
            jnp.einsum(
                "kgqt,qkgd->tkd", grad_scores, grouped_heads, preferred_element_type=jnp.float32
            )
            * inv_root
        )
        grad_values = jnp.einsum(
            "kgqt,qkgd->tkd",
            soft_probs.astype(jnp.bfloat16),
            grouped_gradient,
            preferred_element_type=jnp.float32,
        )
        return (
            running,
            jnp.concatenate(
                [
                    grad_keys.reshape(key_block_index, key_value_width),
                    grad_values.reshape(key_block_index, key_value_width),
                ],
                axis=1,
            ),
        )

    query_running, pair_grads = lax.scan(
        gradient_update,
        jnp.zeros((token_rows, KEY_VALUE_HEADS, group_width, HEAD_SIZE), jnp.float32),
        key_block_list,
    )
    grad_query_rot = query_running.reshape(token_rows, QUERY_HEADS, HEAD_SIZE) * inv_root
    local_gradients = lax.psum_scatter(
        pair_grads.reshape(full_len, 2 * key_value_width).astype(jnp.bfloat16),
        "ctx",
        scatter_dimension=0,
        tiled=True,
    ).astype(jnp.float32)
    rotated_key_gradient = local_gradients[:, :key_value_width].reshape(
        token_rows, KEY_VALUE_HEADS, HEAD_SIZE
    )
    grad_value = local_gradients[:, key_value_width:]
    grad_query, query_gain_part = norm_backward(
        query_raw, query_inverse, query_gain, rotate_back(grad_query_rot, cosines, sine_vals)
    )
    grad_key, key_gain_part = norm_backward(
        unrotated_key, key_inverse, key_gain, rotate_back(rotated_key_gradient, cosines, sine_vals)
    )
    grad_projected = jnp.concatenate(
        [
            grad_query.reshape(token_rows, QUERY_HEADS * HEAD_SIZE),
            grad_key.reshape(token_rows, key_value_width),
            grad_value,
        ],
        axis=1,
    ).astype(jnp.bfloat16)
    grad_normed = times_transposed(grad_projected, qkv_full)
    grad_input_part, attn_gain_part = norm_backward(pack_in, attn_inverse, attn_gain, grad_normed)
    tokens_grad = grad_resid + grad_input_part

    def arrange(values):
        leading = values.shape[:-1]
        last_len = values.shape[-1]
        split_view = values.reshape(
            leading + (fsdp_count, ctx_count, last_len // (fsdp_count * ctx_count))
        )
        return jnp.swapaxes(split_view, -3, -2).reshape(leading + (last_len,))

    qk_sum = jnp.stack([jnp.sum(query_gain_part, axis=(0, 1)), jnp.sum(key_gain_part, axis=(0, 1))])
    qk_major = jnp.transpose(
        qk_sum.reshape(2, fsdp_count, HEAD_SIZE // fsdp_count), (1, 0, 2)
    ).reshape(2 * HEAD_SIZE)
    grad_qkv = transposed_times(arrange(normed_low), grad_projected)
    grad_out = transposed_times(arrange(attended), grad_branch)
    grad_wgate = transposed_times(arrange(normed_ffn_low), grad_gate)
    grad_wup = transposed_times(arrange(normed_ffn_low), grad_up)
    grad_wdown = transposed_times(arrange(hidden), grad_mixed)
    grad_attn_gain = arrange(jnp.sum(attn_gain_part, axis=0))
    grad_ffn_gain = arrange(jnp.sum(ffn_gain_part, axis=0))
    grad_qk_gain = arrange(qk_major)
    pieces = (
        lax.psum_scatter(grad_qkv, ("ctx", "fsdp"), scatter_dimension=0, tiled=True),
        lax.psum_scatter(grad_out, ("ctx", "fsdp"), scatter_dimension=0, tiled=True),
        lax.psum_scatter(grad_wgate, ("ctx", "fsdp"), scatter_dimension=0, tiled=True),
        lax.psum_scatter(grad_wup, ("ctx", "fsdp"), scatter_dimension=0, tiled=True),
        lax.psum_scatter(grad_wdown, ("ctx", "fsdp"), scatter_dimension=0, tiled=True),
        lax.psum_scatter(grad_attn_gain, ("ctx", "fsdp"), scatter_dimension=0, tiled=True),
        lax.psum_scatter(grad_ffn_gain, ("ctx", "fsdp"), scatter_dimension=0, tiled=True),
        lax.psum_scatter(grad_qk_gain, ("ctx", "fsdp"), scatter_dimension=0, tiled=True),
    )
    totals = (
        lax.all_gather(pieces[0].astype(jnp.bfloat16), "ctx", axis=0, tiled=True).astype(
            jnp.float32
        ),
        lax.all_gather(pieces[1].astype(jnp.bfloat16), "ctx", axis=0, tiled=True).astype(
            jnp.float32
        ),
        lax.all_gather(pieces[2].astype(jnp.bfloat16), "ctx", axis=0, tiled=True).astype(
            jnp.float32
        ),
        lax.all_gather(pieces[3].astype(jnp.bfloat16), "ctx", axis=0, tiled=True).astype(
            jnp.float32
        ),
        lax.all_gather(pieces[4].astype(jnp.bfloat16), "ctx", axis=0, tiled=True).astype(
            jnp.float32
        ),
        lax.all_gather(pieces[5].astype(jnp.bfloat16), "ctx", axis=0, tiled=True).astype(
            jnp.float32
        ),
        lax.all_gather(pieces[6].astype(jnp.bfloat16), "ctx", axis=0, tiled=True).astype(
            jnp.float32
        ),
        lax.all_gather(pieces[7].astype(jnp.bfloat16), "ctx", axis=0, tiled=True).astype(
            jnp.float32
        ),
    )
    qk_shard = totals[7].reshape(2, HEAD_SIZE // fsdp_count)
    return (
        mixed_out[None],
        tokens_grad[None],
        totals[0],
        totals[1],
        totals[2],
        totals[3],
        totals[4],
        totals[5],
        totals[6],
        qk_shard,
    )


def solution(mesh):
    return jax.shard_map(
        per_device,
        mesh=mesh,
        in_specs=(
            P("fsdp", "ctx", None),
            P("fsdp", "ctx", None),
            P("fsdp", None),
            P(),
            P("fsdp", None),
            P("fsdp", None),
            P("fsdp", None),
            P("fsdp", None),
            P("fsdp", None),
            P("fsdp"),
            P("fsdp"),
            P(None, "fsdp"),
        ),
        out_specs=(
            P("fsdp", "ctx", None),
            P("fsdp", "ctx", None),
            P("fsdp", None),
            P("fsdp", None),
            P("fsdp", None),
            P("fsdp", None),
            P("fsdp", None),
            P("fsdp"),
            P("fsdp"),
            P(None, "fsdp"),
        ),
        check_vma=False,
    )
```

profile of v0, /device:TPU:0, one launch (start us, length us, event | category | flops | bytes accessed | tf_op | source)
XLA Modules:
  0.0 1678.6 jit_solution(975257978420920304)
XLA Ops:
  8.7 13.6 all-gather
  22.9 10.2 all-gather.1
  39.7 5.8 fusion.96
  46.9 80.8 %all-gather.15.cloned.1.call-done = bf16[2048,1536]{1,0:T(8,128)(2,1)} async-done(((bf16[512,1536]{1,0:T(8,128)(2,1)}), bf16[2048,1536]{1,0:T(8,128)(2,1)}) %all-gather.15.cloned.1.call-update) | async-done | bytes 6291472 | tf_op jit(solution)/shard_map/all_gather | solution.py:90
  127.7 4.6 fusion.79
  137.0 12.5 all-gather.2
  153.3 7.1 all-gather.17.cloned.1.call-done
  171.6 40.3 %while.49 = (s32[]{:T(128)}, f32[4,4,256]{2,1,0:T(4,128)S(1)}, f32[4,4,256]{2,1,0:T(4,128)S(1)}, s32[256]{0:T(256)S(1)}, s32[4,512]{1,0:T(4,128)S(1)}, /*index=5...) while((s32[]{:T(128)}, f32[4,4,256]{2,1,0:T(4,128)S(1)}, ...), condition=%wide.region_7.8_spmd.clone, body=%wide.region_4.7_spmd.clone.sunk | while | flops 283529216 | bytes 18184328 | solution.py:180
  171.9 4.6 fusion.177
  176.5 5.2 exponential_reduce_fusion.2
  181.9 4.6 fusion.177
  186.6 5.2 exponential_reduce_fusion.2
  192.1 4.6 fusion.177
  196.7 5.1 exponential_reduce_fusion.2
  202.1 4.6 fusion.177
  206.8 5.1 exponential_reduce_fusion.2
  211.9 20.5 %while.50 = (s32[]{:T(128)}, f32[256,4,4,64]{0,3,2,1:T(8,128)}, bf16[4,512,4,64]{1,3,2,0:T(8,128)(2,1)S(1)}, s32[256]{0:T(256)S(1)}, s32[4,512]{1,0:T(4,128)S(1)...) while((s32[]{:T(128)}, f32[256,4,4,64]{0,3,2,1:T(8,128)}, ...), condition=%wide.region_9.10_spmd.clone, body=%wide.region_8.9_spmd.clone.sunk | while | flops 548274176 | bytes 3456658 | solution.py:198
  216.3 5.2 fusion.183
  221.7 5.2 fusion.183
  227.1 5.2 fusion.183
  234.5 8.2 all-gather.19.cloned.1.call-done
  248.1 75.3 %all-gather.21.cloned.1.call-done = bf16[2048,1024]{1,0:T(8,128)(2,1)} async-done(((bf16[512,1024]{1,0:T(8,128)(2,1)}), bf16[2048,1024]{1,0:T(8,128)(2,1)}) %all-gather.21.cloned.1.call-update) | async-done | bytes 4194320 | tf_op jit(solution)/shard_map/all_gather | solution.py:96
  323.4 4.7 fusion.108
  328.2 75.9 %all-gather.23.cloned.1.call-done = bf16[2048,1024]{1,0:T(8,128)(2,1)} async-done(((bf16[512,1024]{1,0:T(8,128)(2,1)}), bf16[2048,1024]{1,0:T(8,128)(2,1)}) %all-gather.23.cloned.1.call-update) | async-done | bytes 4194320 | tf_op jit(solution)/shard_map/all_gather | solution.py:97
  404.1 4.7 fusion.109
  408.8 76.0 %all-gather.25.cloned.1.call-done = bf16[1024,2048]{1,0:T(8,128)(2,1)} async-done(((bf16[256,2048]{1,0:T(8,128)(2,1)}), bf16[1024,2048]{1,0:T(8,128)(2,1)}) %all-gather.25.cloned.1.call-update) | async-done | bytes 4194320 | tf_op jit(solution)/shard_map/all_gather | solution.py:98
  484.8 5.7 multiply_convert_fusion.2
  500.0 22.7 %while.51 = (s32[]{:T(128)}, f32[4,4,256]{2,1,0:T(4,128)S(1)}, s32[256]{0:T(256)S(1)}, s32[4,512]{1,0:T(4,128)S(1)}, s32[4,512]{1,0:T(4,128)S(1)}, /*index=5*/s3...) while((s32[]{:T(128)}, f32[4,4,256]{2,1,0:T(4,128)S(1)}, ...), condition=%wide.region_14.15_spmd.clone, body=%wide.region_12.14_spmd.clone.sunk | while | flops 549851136 | bytes 18725024 | solution.py:238
  522.7 69.2 %while.52 = (s32[]{:T(128)}, f32[256,4,4,64]{0,3,2,1:T(8,128)S(1)}, bf16[4,512,512]{1,2,0:T(8,128)(2,1)}, bf16[4,512,4,64]{1,3,2,0:T(8,128)(2,1)S(1)}, s32[256]{...) while((s32[]{:T(128)}, f32[256,4,4,64]{0,3,2,1:T(8,128)S(1)}, ...), condition=%wide.region_16.17_spmd.clone, body=%wide.region_15.16_spmd.clone.sunk | while | flops 1361182720 | bytes 94959864 | solution.py:276
  532.9 4.9 fusion.203
  542.6 4.5 fusion.201
  550.2 4.9 fusion.203
  567.5 4.9 fusion.203
  584.8 4.9 fusion.203
  597.2 6.2 fusion.87
  612.8 4.5 fusion.112
  649.7 7.7 fusion.90
  657.5 166.4 %reduce-scatter.11.cloned.1.call-done = f32[32,2048]{1,0:T(8,128)} async-done(((f32[1024,2048]{1,0:T(8,128)}), f32[32,2048]{1,0:T(8,128)}) %reduce-scatter.11.cloned.1.call-update) | async-done | bytes 262160 | tf_op jit(solution)/shard_map/reduce_scatter | solution.py:332
  825.6 184.0 %reduce-scatter.13.cloned.1.call-done = f32[64,1024]{1,0:T(8,128)} async-done(((f32[2048,1024]{1,0:T(8,128)}), f32[64,1024]{1,0:T(8,128)}) %reduce-scatter.13.cloned.1.call-update) | async-done | bytes 262160 | tf_op jit(solution)/shard_map/reduce_scatter | solution.py:333
  1011.3 183.9 %reduce-scatter.15.cloned.1.call-done = f32[64,1024]{1,0:T(8,128)} async-done(((f32[2048,1024]{1,0:T(8,128)}), f32[64,1024]{1,0:T(8,128)}) %reduce-scatter.15.cloned.1.call-update) | async-done | bytes 262160 | tf_op jit(solution)/shard_map/reduce_scatter | solution.py:334
  1196.9 184.0 %reduce-scatter.17.cloned.1.call-done = f32[32,2048]{1,0:T(8,128)} async-done(((f32[1024,2048]{1,0:T(8,128)}), f32[32,2048]{1,0:T(8,128)}) %reduce-scatter.17.cloned.1.call-update) | async-done | bytes 262160 | tf_op jit(solution)/shard_map/reduce_scatter | solution.py:335
  1382.6 156.8 %reduce-scatter.9.cloned.1.call-done = f32[64,1536]{1,0:T(8,128)} async-done(((f32[2048,1536]{1,0:T(8,128)}), f32[64,1536]{1,0:T(8,128)}) %reduce-scatter.9.cloned.1.call-update) | async-done | bytes 393232 | tf_op jit(solution)/shard_map/reduce_scatter | solution.py:331
  1543.4 4.6 fusion.61
  1548.1 6.2 fusion.73
  1554.9 40.2 %all-reduce.6 = (bf16[2048]{0:T(1024)(128)(2,1)S(1)}, bf16[2048]{0:T(1024)(128)(2,1)S(1)}, bf16[128]{0:T(256)(128)(2,1)S(1)}) all-reduce(f32[2048]{0:T(1024)S(1)} %reshape.630, f32[2048]{0:T(1024)S(1)} %reshape.632, f32[128]{0:T(128)S(1)} %reshape.633), channel_id=8, replica_groups=mesh['ctx'=8,'fsdp'=4] {'ctx','fsdp'}, use_global_device_ids=true, to_apply=%region_27.28.clone | all-reduce | flops 4224 | bytes 25344
  1595.9 12.7 all-reduce.7
  1622.3 17.8 %all-gather.35.cloned.1.call-done = bf16[256,2048]{1,0:T(8,128)(2,1)} async-done(((bf16[32,2048]{1,0:T(8,128)(2,1)}), bf16[256,2048]{1,0:T(8,128)(2,1)}) %all-gather.35.cloned.1.call-update) | async-done | bytes 1048592 | tf_op jit(solution)/shard_map/all_gather | solution.py:353
  1642.9 25.1 %all-gather.27.cloned.1.call-done = bf16[512,1536]{1,0:T(8,128)(2,1)} async-done(((bf16[64,1536]{1,0:T(8,128)(2,1)}), bf16[512,1536]{1,0:T(8,128)(2,1)}) %all-gather.27.cloned.1.call-update) | async-done | bytes 1572880 | tf_op jit(solution)/shard_map/all_gather | solution.py:341
  (384 shorter events, 196.5 us)
Async XLA Ops:
  7.2 39.2 %copy-start.7 = (bf16[1,256,2048]{2,1,0:T(8,128)(2,1)S(1)}, bf16[1,256,2048]{2,1,0:T(8,128)(2,1)}, u32[]{:S(2)}) copy-start(bf16[1,256,2048]{2,1,0:T(8,128)(2,1)} %param.22) | copy-start | bytes 3145732
  7.2 120.5 %all-gather.15.cloned.1.call-start = ((), (), s32[]{:S(2)}) async-start(), calls=%async_computation.6 | async-start | bytes 7864320 | tf_op jit(solution)/shard_map/all_gather | solution.py:90
  7.9 152.5 %all-gather.17.cloned.1.call-start = ((), (), s32[]{:S(2)}) async-start(), calls=%async_computation.7 | async-start | bytes 2359296 | tf_op jit(solution)/shard_map/all_gather | solution.py:142
  22.9 109.4 %copy-start.46 = (f32[4,1,512]{2,1,0:T(1,128)}, f32[4,1,512]{2,1,0:T(1,128)S(1)}, u32[]{:S(2)}) copy-start(f32[4,1,512]{2,1,0:T(1,128)S(1)} %convert_element_type.198) | copy-start | bytes 24580
  46.6 85.9 %copy-start.50 = (f32[64]{0:T(128)}, f32[64]{0:T(128)S(1)}, u32[]{:S(2)}) copy-start(f32[64]{0:T(128)S(1)} %get-tuple-element.802) | copy-start | bytes 772
  46.7 105.8 %copy-start.52 = (f32[64]{0:T(128)}, f32[64]{0:T(128)S(1)}, u32[]{:S(2)}) copy-start(f32[64]{0:T(128)S(1)} %get-tuple-element.801) | copy-start | bytes 772
  46.7 85.6 %copy-start.48 = (f32[256]{0:T(256)}, f32[256]{0:T(256)S(1)}, u32[]{:S(2)}) copy-start(f32[256]{0:T(256)S(1)} %add_rsqrt_fusion.3) | copy-start | bytes 3076
  46.9 105.8 %copy-start.29 = (f32[256,32]{0,1:T(8,128)}, f32[256,32]{0,1:T(8,128)S(1)}, u32[]{:S(2)}) copy-start(f32[256,32]{0,1:T(8,128)S(1)} %get-tuple-element.799) | copy-start | bytes 98308
  46.9 105.8 %copy-start.31 = (f32[256,32]{0,1:T(8,128)}, f32[256,32]{0,1:T(8,128)S(1)}, u32[]{:S(2)}) copy-start(f32[256,32]{0,1:T(8,128)S(1)} %get-tuple-element.800) | copy-start | bytes 98308
  132.3 17.3 %copy-start.17 = (f32[256,1536]{1,0:T(8,128)}, f32[256,1536]{1,0:T(8,128)S(1)}, u32[]{:S(2)}) copy-start(f32[256,1536]{1,0:T(8,128)S(1)} %fusion.79) | copy-start | bytes 4718596
  134.3 15.1 copy-start.54
  134.3 15.1 copy-start.55
  134.3 108.4 %all-gather.19.cloned.1.call-start = ((), (), s32[]{:S(2)}) async-start(), calls=%async_computation.8 | async-start | bytes 5242880 | tf_op jit(solution)/shard_map/all_gather | solution.py:91
  135.1 188.4 %all-gather.21.cloned.1.call-start = ((), (), s32[]{:S(2)}) async-start(), calls=%async_computation.9 | async-start | bytes 5242880 | tf_op jit(solution)/shard_map/all_gather | solution.py:96
  135.7 268.5 %all-gather.23.cloned.1.call-start = ((), (), s32[]{:S(2)}) async-start(), calls=%async_computation.10 | async-start | bytes 5242880 | tf_op jit(solution)/shard_map/all_gather | solution.py:97
  136.2 348.6 %all-gather.25.cloned.1.call-start = ((), (), s32[]{:S(2)}) async-start(), calls=%async_computation.11 | async-start | bytes 5242880 | tf_op jit(solution)/shard_map/all_gather | solution.py:98
  136.8 507.2 %reduce-scatter.7.cloned.1.call-start = ((), (), s32[]{:S(2)}) async-start(), calls=%async_computation.12 | async-start | bytes 2359296 | tf_op jit(solution)/shard_map/reduce_scatter | solution.py:282
  232.5 10.3 copy-start.11
  232.5 10.3 copy-start.14
  234.5 12.1 copy-start.15
  246.6 248.9 %copy-start.3 = (f32[256,2048]{1,0:T(8,128)}, f32[256,2048]{1,0:T(8,128)S(1)}, u32[]{:S(2)}) copy-start(f32[256,2048]{1,0:T(8,128)S(1)} %get-tuple-element.820) | copy-start | bytes 6291460
  484.8 5.7 copy-start.57
  499.9 22.8 %copy-start.2 = (f32[256,4,4,64]{0,3,2,1:T(8,128)S(1)}, f32[256,4,4,64]{0,3,2,1:T(8,128)}, u32[]{:S(2)}) copy-start(f32[256,4,4,64]{0,3,2,1:T(8,128)} %custom-call.4) | copy-start | bytes 3145732
  525.3 4.5 copy-start.1
  532.9 4.9 copy-start
  542.6 4.5 copy-start.1
  550.2 4.9 copy-start
  567.5 4.9 copy-start
  584.8 4.9 copy-start
  596.1 227.8 %reduce-scatter.11.cloned.1.call-start = ((), (), s32[]{:S(2)}) async-start(), calls=%async_computation.15 | async-start | bytes 8650752 | tf_op jit(solution)/shard_map/reduce_scatter | solution.py:332
  603.4 406.2 %reduce-scatter.13.cloned.1.call-start = ((), (), s32[]{:S(2)}) async-start(), calls=%async_computation.17 | async-start | bytes 8650752 | tf_op jit(solution)/shard_map/reduce_scatter | solution.py:333
  611.8 583.4 %reduce-scatter.15.cloned.1.call-start = ((), (), s32[]{:S(2)}) async-start(), calls=%async_computation.19 | async-start | bytes 8650752 | tf_op jit(solution)/shard_map/reduce_scatter | solution.py:334
  617.4 763.6 %reduce-scatter.17.cloned.1.call-start = ((), (), s32[]{:S(2)}) async-start(), calls=%async_computation.21 | async-start | bytes 8650752 | tf_op jit(solution)/shard_map/reduce_scatter | solution.py:335
  623.3 916.1 %reduce-scatter.9.cloned.1.call-start = ((), (), s32[]{:S(2)}) async-start(), calls=%async_computation.13 | async-start | bytes 12976128 | tf_op jit(solution)/shard_map/reduce_scatter | solution.py:331
  640.8 5.1 copy-start.24
  649.6 7.7 copy-start.34
  657.4 883.8 %copy-start.58 = (u32[32]{0:T(128)S(1)}, u32[32]{0:T(128)}, u32[]{:S(2)}) copy-start(u32[32]{0:T(128)} %constant.241) | copy-start | bytes 388
  657.4 885.7 %copy-start.45 = (f32[2048]{0:T(1024)S(1)}, f32[2048]{0:T(1024)}, u32[]{:S(2)}) copy-start(f32[2048]{0:T(1024)} %get-tuple-element.648) | copy-start | bytes 24580
  657.4 886.0 %copy-start.4 = (f32[256,2048]{1,0:T(8,128)S(1)}, f32[256,2048]{1,0:T(8,128)}, u32[]{:S(2)}) copy-start(f32[256,2048]{1,0:T(8,128)} %copy-done.3) | copy-start | bytes 6291460
  657.4 956.5 %all-gather.29.cloned.1.call-start = ((), (), s32[]{:S(2)}) async-start(), calls=%async_computation.16 | async-start | bytes 1179648 | tf_op jit(solution)/shard_map/all_gather | solution.py:344
  825.6 791.2 %all-gather.31.cloned.1.call-start = ((), (), s32[]{:S(2)}) async-start(), calls=%async_computation.18 | async-start | bytes 1179648 | tf_op jit(solution)/shard_map/all_gather | solution.py:347
  1011.3 608.3 %all-gather.33.cloned.1.call-start = ((), (), s32[]{:S(2)}) async-start(), calls=%async_computation.20 | async-start | bytes 1179648 | tf_op jit(solution)/shard_map/all_gather | solution.py:350
  1196.8 443.3 %all-gather.35.cloned.1.call-start = ((), (), s32[]{:S(2)}) async-start(), calls=%async_computation.22 | async-start | bytes 1179648 | tf_op jit(solution)/shard_map/all_gather | solution.py:353
  1382.6 285.5 %all-gather.27.cloned.1.call-start = ((), (), s32[]{:S(2)}) async-start(), calls=%async_computation.14 | async-start | bytes 1769472 | tf_op jit(solution)/shard_map/all_gather | solution.py:341
  1543.4 4.7 copy-start.25
  1543.4 4.7 copy-start.35
  1543.4 4.7 copy-start.47
  1548.1 62.4 %copy-start.6 = (f32[256,2048]{1,0:T(8,128)S(1)}, f32[256,2048]{1,0:T(8,128)}, u32[]{:S(2)}) copy-start(f32[256,2048]{1,0:T(8,128)} %copy-done.5) | copy-start | bytes 6291460
  (34 other events, 77.5 us)
Sparse Core Ops, SparseCore 0:
  9.6 118.0 all-gather.14
  134.4 25.9 all-gather.16
  162.0 80.7 all-gather.18
  244.2 79.2 all-gather.20
  324.9 79.2 all-gather.22
  405.5 79.2 all-gather.24
  596.2 39.5 reduce-scatter.6
  638.2 185.7 reduce-scatter.10
  826.2 183.3 reduce-scatter.12
  1011.8 183.3 reduce-scatter.14
  1197.5 183.3 reduce-scatter.16
  1386.8 152.5 reduce-scatter.8
  1541.9 22.7 all-gather.28
  1566.4 23.2 all-gather.30
  1591.5 23.4 all-gather.32
  1616.7 23.3 all-gather.34
  1642.5 25.5 all-gather.26
where the time goes:
time: 1680 us
  waiting for transfers between devices  1240 us (74%)
  matrix products  191 us (11%)
  blocking collectives  89.2 us (5%)
  other arithmetic  81.4 us (5%)
  local copies, waits for them, and re-layouts  53.6 us (3%)
  between operations  16.8 us (1%)
    reduce_scatter x1, waiting for transfers between devices, per_device(): lax.psum_scatter(grad_wdown, ('ctx', 'fsdp'), scatter_dimension=0, tiled=...  184 us
    reduce_scatter x1, waiting for transfers between devices, per_device(): lax.psum_scatter(grad_wgate, ('ctx', 'fsdp'), scatter_dimension=0, tiled=...  184 us
    reduce_scatter x1, waiting for transfers between devices, per_device(): lax.psum_scatter(grad_wup, ('ctx', 'fsdp'), scatter_dimension=0, tiled=True)  184 us
    reduce_scatter x1, waiting for transfers between devices, per_device(): lax.psum_scatter(grad_out, ('ctx', 'fsdp'), scatter_dimension=0, tiled=True)  166 us
    reduce_scatter x1, waiting for transfers between devices, per_device(): lax.psum_scatter(grad_qkv, ('ctx', 'fsdp'), scatter_dimension=0, tiled=True)  157 us
    all_gather x1, waiting for transfers between devices, per_device(): lax.all_gather(query_key_value_weight, 'fsdp', axis=0, tiled=True)  80.8 us
    all_gather x1, waiting for transfers between devices, per_device(): lax.all_gather(w_down, 'fsdp', axis=0, tiled=True)  76 us
    all_gather x1, waiting for transfers between devices, per_device(): lax.all_gather(w_up, 'fsdp', axis=0, tiled=True)  75.9 us
  transfers between devices with their start and end apart: 17, of which 13 were waited for; matrix products, arithmetic and copies ran while one was open for 12% of the time, Pallas kernels for 0%

commit v1 on v0

--- a/solution.py
+++ b/solution.py
@@ -9,6 +9,22 @@
 HEAD_SIZE = 64
 EPSILON = 1e-06
 THETA = 10000.0
+
+
+def ring_gather(x, axis, dim):
+    ways, here, step = (lax.axis_size(axis), lax.axis_index(axis), x.shape[dim])
+    dims = [n * ways if d == dim else n for d, n in enumerate(x.shape)]
+    full = lax.dynamic_update_slice_in_dim(jnp.zeros(dims, x.dtype), x, here * step, axis=dim)
+    going_up = going_down = x
+    for far in range(1, ways // 2 + 1):
+        going_up = lax.ppermute(going_up, axis, [(d, (d + 1) % ways) for d in range(ways)])
+        full = lax.dynamic_update_slice_in_dim(full, going_up, (here - far) % ways * step, axis=dim)
+        if 2 * far < ways:
+            going_down = lax.ppermute(going_down, axis, [(d, (d - 1) % ways) for d in range(ways)])
+            full = lax.dynamic_update_slice_in_dim(
+                full, going_down, (here + far) % ways * step, axis=dim
+            )
+    return full
 
 
 def times_transposed(left, right):
@@ -95,7 +111,7 @@
     gate_full, up_full, down_full, ffn_gathered = (
         lax.all_gather(w_gate, "fsdp", axis=0, tiled=True),
         lax.all_gather(w_up, "fsdp", axis=0, tiled=True),
-        lax.all_gather(w_down, "fsdp", axis=0, tiled=True),
+        ring_gather(w_down, "fsdp", 0),
         lax.all_gather(gain_ffn, "fsdp", axis=0, tiled=True),
     )
     attn_gain = attn_gathered.astype(jnp.float32)

time: 1680 us -> 1620 us (0.964)
  waiting for transfers between devices: 1240 us -> 1110 us
  blocking collectives: 89.2 us -> 170 us
  matrix products: 191 us -> 164 us
    all_gather x1, blocking collectives: 12.5 us -> 93.6 us  [per_device(): lax.all_gather(gain_ffn, 'fsdp', axis=0, tiled=True)]
    all_gather x1 -> x0, waiting for transfers between devices: 76 us -> none  [per_device(): lax.all_gather(w_down, 'fsdp', axis=0, tiled=True)]
    all_gather x1, waiting for transfers between devices: 75.3 us -> 11 us  [per_device(): lax.all_gather(w_gate, 'fsdp', axis=0, tiled=True)]
    ppermute x0 -> x3, waiting for transfers between devices: none -> 24.1 us  [the longest x2 24.1 us: ring_gather(): lax.ppermute(going_up, axis, [(d, (d + 1) % ways) for d in range(ways)])]
  transfers between devices with their start and end apart: 17 -> 19, of which waited for: 13 -> 11; matrix products, arithmetic and copies ran while one was open for 12% -> 12% of each run, Pallas kernels for 0% -> 0%
where the time goes in v1:
time: 1620 us
  waiting for transfers between devices  1110 us (69%)
  blocking collectives  170 us (10%)
  matrix products  164 us (10%)
  other arithmetic  84.1 us (5%)
  local copies, waits for them, and re-layouts  62.6 us (4%)
  between operations  16.9 us (1%)
    reduce_scatter x1, waiting for transfers between devices, per_device(): lax.psum_scatter(grad_wup, ('ctx', 'fsdp'), scatter_dimension=0, tiled=True)  184 us
    reduce_scatter x1, waiting for transfers between devices, per_device(): lax.psum_scatter(grad_wgate, ('ctx', 'fsdp'), scatter_dimension=0, tiled=...  184 us
    reduce_scatter x1, waiting for transfers between devices, per_device(): lax.psum_scatter(grad_wdown, ('ctx', 'fsdp'), scatter_dimension=0, tiled=...  184 us
    reduce_scatter x1, waiting for transfers between devices, per_device(): lax.psum_scatter(grad_out, ('ctx', 'fsdp'), scatter_dimension=0, tiled=True)  168 us
    reduce_scatter x1, waiting for transfers between devices, per_device(): lax.psum_scatter(grad_qkv, ('ctx', 'fsdp'), scatter_dimension=0, tiled=True)  157 us
    all_gather x1, blocking collectives, per_device(): lax.all_gather(gain_ffn, 'fsdp', axis=0, tiled=True)  93.6 us
    all_gather x1, waiting for transfers between devices, per_device(): lax.all_gather(query_key_value_weight, 'fsdp', axis=0, tiled=True)  79.4 us
    all_gather x1, waiting for transfers between devices, per_device(): lax.all_gather(w_up, 'fsdp', axis=0, tiled=True)  75.9 us
  transfers between devices with their start and end apart: 19, of which 11 were waited for; matrix products, arithmetic and copies ran while one was open for 12% of the time, Pallas kernels for 0%

profile of v1, /device:TPU:0, one launch (start us, length us, event | category | flops | bytes accessed | tf_op | source)
XLA Modules:
  0.0 1616.3 jit_solution(630023891821323612)
XLA Ops:
  8.6 13.6 all-gather
  22.9 10.2 all-gather.1
  35.2 4.4 compare_select_fusion.1
  39.8 5.8 fusion.95
  48.3 79.4 %all-gather.14.cloned.1.call-done = bf16[2048,1536]{1,0:T(8,128)(2,1)} async-done(((bf16[512,1536]{1,0:T(8,128)(2,1)}), bf16[2048,1536]{1,0:T(8,128)(2,1)}) %all-gather.14.cloned.1.call-update) | async-done | bytes 6291472 | tf_op jit(solution)/shard_map/all_gather | solution.py:106
  127.7 5.0 fusion.79
  135.4 3.8 collective-permute-start.1
  139.3 24.1 %collective-permute-done = bf16[256,2048]{1,0:T(8,128)(2,1)} collective-permute-done((bf16[256,2048]{1,0:T(8,128)(2,1)S(1)}, bf16[256,2048]{1,0:T(8,128)(2,1)}, u32[]{:S(2)}, u32[]{:S(2)}) %collective-permute-start) | collective-permute-done | bytes 1048608 | tf_op jit(solution)/shard_map/ppermute | solution.py:20
  163.6 93.6 %all-gather.2 = bf16[4,1,512]{2,1,0:T(2,128)(2,1)S(1)} all-gather(bf16[1,1,512]{2,1,0:T(2,128)(2,1)S(1)} %reshape.717), channel_id=1, replica_groups=mesh['ctx'=8,'fsdp'=4] {'fsdp'}, dimensions={0}, use_global_device_ids=true | all-gather | bytes 5120 | tf_op jit(solution)/shard_map/all_gather | solution.py:115
  271.7 40.2 %while.49 = (s32[]{:T(128)}, f32[4,4,256]{2,1,0:T(4,128)S(1)}, f32[4,4,256]{2,1,0:T(4,128)S(1)}, s32[256]{0:T(256)S(1)}, s32[4,512]{1,0:T(4,128)S(1)}, /*index=5...) while((s32[]{:T(128)}, f32[4,4,256]{2,1,0:T(4,128)S(1)}, ...), condition=%wide.region_7.8_spmd.clone, body=%wide.region_4.7_spmd.clone.sunk | while | flops 283529216 | bytes 18184320 | solution.py:196
  272.0 4.6 fusion.176
  276.6 5.1 exponential_reduce_fusion.2
  282.0 4.6 fusion.176
  286.7 5.1 exponential_reduce_fusion.2
  292.0 4.6 fusion.176
  296.7 5.1 exponential_reduce_fusion.2
  302.1 4.6 fusion.176
  306.7 5.2 exponential_reduce_fusion.2
  316.7 20.4 %while.50 = (s32[]{:T(128)}, f32[256,4,4,64]{0,3,2,1:T(8,128)}, bf16[4,512,4,64]{1,3,2,0:T(8,128)(2,1)S(1)}, s32[256]{0:T(256)S(1)}, s32[4,512]{1,0:T(4,128)S(1)...) while((s32[]{:T(128)}, f32[256,4,4,64]{0,3,2,1:T(8,128)}, ...), condition=%wide.region_9.10_spmd.clone, body=%wide.region_8.9_spmd.clone.sunk | while | flops 548274176 | bytes 3456139 | solution.py:214
  316.9 3.9 fusion.182
  321.1 5.1 fusion.182
  326.4 5.1 fusion.182
  331.8 5.1 fusion.182
  339.2 4.0 multiply_reduce_fusion.2
  344.7 11.0 all-gather.20.cloned.1.call-done
  355.7 4.7 fusion.107
  360.4 75.9 %all-gather.22.cloned.1.call-done = bf16[2048,1024]{1,0:T(8,128)(2,1)} async-done(((bf16[512,1024]{1,0:T(8,128)(2,1)}), bf16[2048,1024]{1,0:T(8,128)(2,1)}) %all-gather.22.cloned.1.call-update) | async-done | bytes 4194320 | tf_op jit(solution)/shard_map/all_gather | solution.py:113
  436.4 3.9 fusion.108
  452.7 22.7 %while.51 = (s32[]{:T(128)}, f32[4,4,256]{2,1,0:T(4,128)S(1)}, s32[256]{0:T(256)S(1)}, s32[4,512]{1,0:T(4,128)S(1)}, s32[4,512]{1,0:T(4,128)S(1)}, /*index=5*/s3...) while((s32[]{:T(128)}, f32[4,4,256]{2,1,0:T(4,128)S(1)}, ...), condition=%wide.region_14.15_spmd.clone, body=%wide.region_12.14_spmd.clone.sunk | while | flops 549851136 | bytes 18725524 | solution.py:254
  475.4 54.1 %while.52 = (s32[]{:T(128)}, f32[256,4,4,64]{0,3,2,1:T(8,128)S(1)}, bf16[4,512,512]{1,2,0:T(8,128)(2,1)}, bf16[4,512,4,64]{1,3,2,0:T(8,128)(2,1)S(1)}, s32[256]{...) while((s32[]{:T(128)}, f32[256,4,4,64]{0,3,2,1:T(8,128)S(1)}, ...), condition=%wide.region_16.17_spmd.clone, body=%wide.region_15.16_spmd.clone.sunk | while | flops 1361182720 | bytes 61406404 | solution.py:292
  529.5 4.2 copy.202
  533.8 6.2 fusion.86
  543.9 4.5 fusion.110
  549.4 4.5 fusion.111
  555.3 4.5 fusion.81
  585.8 7.7 fusion.89
  593.6 167.9 %reduce-scatter.11.cloned.1.call-done = f32[32,2048]{1,0:T(8,128)} async-done(((f32[1024,2048]{1,0:T(8,128)}), f32[32,2048]{1,0:T(8,128)}) %reduce-scatter.11.cloned.1.call-update) | async-done | bytes 262160 | tf_op jit(solution)/shard_map/reduce_scatter | solution.py:348
  763.3 184.0 %reduce-scatter.13.cloned.1.call-done = f32[64,1024]{1,0:T(8,128)} async-done(((f32[2048,1024]{1,0:T(8,128)}), f32[64,1024]{1,0:T(8,128)}) %reduce-scatter.13.cloned.1.call-update) | async-done | bytes 262160 | tf_op jit(solution)/shard_map/reduce_scatter | solution.py:349
  949.0 184.0 %reduce-scatter.15.cloned.1.call-done = f32[64,1024]{1,0:T(8,128)} async-done(((f32[2048,1024]{1,0:T(8,128)}), f32[64,1024]{1,0:T(8,128)}) %reduce-scatter.15.cloned.1.call-update) | async-done | bytes 262160 | tf_op jit(solution)/shard_map/reduce_scatter | solution.py:350
  1134.7 183.9 %reduce-scatter.17.cloned.1.call-done = f32[32,2048]{1,0:T(8,128)} async-done(((f32[1024,2048]{1,0:T(8,128)}), f32[32,2048]{1,0:T(8,128)}) %reduce-scatter.17.cloned.1.call-update) | async-done | bytes 262160 | tf_op jit(solution)/shard_map/reduce_scatter | solution.py:351
  1320.3 156.9 %reduce-scatter.9.cloned.1.call-done = f32[64,1536]{1,0:T(8,128)} async-done(((f32[2048,1536]{1,0:T(8,128)}), f32[64,1536]{1,0:T(8,128)}) %reduce-scatter.9.cloned.1.call-update) | async-done | bytes 393232 | tf_op jit(solution)/shard_map/reduce_scatter | solution.py:347
  1481.2 4.6 fusion.61
  1486.2 6.3 fusion.73
  1492.7 40.2 %all-reduce.6 = (bf16[2048]{0:T(1024)(128)(2,1)S(1)}, bf16[2048]{0:T(1024)(128)(2,1)S(1)}, bf16[128]{0:T(256)(128)(2,1)S(1)}) all-reduce(f32[2048]{0:T(1024)S(1)} %reshape.630, f32[2048]{0:T(1024)S(1)} %reshape.632, f32[128]{0:T(128)S(1)} %reshape.633), channel_id=8, replica_groups=mesh['ctx'=8,'fsdp'=4] {'ctx','fsdp'}, use_global_device_ids=true, to_apply=%region_27.28.clone | all-reduce | flops 4224 | bytes 25344
  1533.8 12.7 all-reduce.7
  1548.3 3.5 fusion.69
  1560.2 17.6 %all-gather.32.cloned.1.call-done = bf16[256,2048]{1,0:T(8,128)(2,1)} async-done(((bf16[32,2048]{1,0:T(8,128)(2,1)}), bf16[256,2048]{1,0:T(8,128)(2,1)}) %all-gather.32.cloned.1.call-update) | async-done | bytes 1048592 | tf_op jit(solution)/shard_map/all_gather | solution.py:369
  1580.6 25.1 %all-gather.24.cloned.1.call-done = bf16[512,1536]{1,0:T(8,128)(2,1)} async-done(((bf16[64,1536]{1,0:T(8,128)(2,1)}), bf16[512,1536]{1,0:T(8,128)(2,1)}) %all-gather.24.cloned.1.call-update) | async-done | bytes 1572880 | tf_op jit(solution)/shard_map/all_gather | solution.py:357
  (380 shorter events, 182.1 us)
Async XLA Ops:
  7.2 120.5 %all-gather.14.cloned.1.call-start = ((), (), s32[]{:S(2)}) async-start(), calls=%async_computation.6 | async-start | bytes 7864320 | tf_op jit(solution)/shard_map/all_gather | solution.py:106
  7.9 257.4 %all-gather.16.cloned.1.call-start = ((), (), s32[]{:S(2)}) async-start(), calls=%async_computation.7 | async-start | bytes 2359296 | tf_op jit(solution)/shard_map/all_gather | solution.py:158
  22.9 109.7 %copy-start.42 = (f32[4,1,512]{2,1,0:T(1,128)}, f32[4,1,512]{2,1,0:T(1,128)S(1)}, u32[]{:S(2)}) copy-start(f32[4,1,512]{2,1,0:T(1,128)S(1)} %convert_element_type.198) | copy-start | bytes 24580
  48.0 85.0 %copy-start.46 = (f32[64]{0:T(128)}, f32[64]{0:T(128)S(1)}, u32[]{:S(2)}) copy-start(f32[64]{0:T(128)S(1)} %get-tuple-element.802) | copy-start | bytes 772
  48.0 216.4 %copy-start.48 = (f32[64]{0:T(128)}, f32[64]{0:T(128)S(1)}, u32[]{:S(2)}) copy-start(f32[64]{0:T(128)S(1)} %get-tuple-element.801) | copy-start | bytes 772
  48.0 84.6 %copy-start.44 = (f32[256]{0:T(256)}, f32[256]{0:T(256)S(1)}, u32[]{:S(2)}) copy-start(f32[256]{0:T(256)S(1)} %add_rsqrt_fusion.3) | copy-start | bytes 3076
  48.3 216.4 %copy-start.27 = (f32[256,32]{0,1:T(8,128)}, f32[256,32]{0,1:T(8,128)S(1)}, u32[]{:S(2)}) copy-start(f32[256,32]{0,1:T(8,128)S(1)} %get-tuple-element.799) | copy-start | bytes 98308
  48.3 216.4 %copy-start.29 = (f32[256,32]{0,1:T(8,128)}, f32[256,32]{0,1:T(8,128)S(1)}, u32[]{:S(2)}) copy-start(f32[256,32]{0,1:T(8,128)S(1)} %get-tuple-element.800) | copy-start | bytes 98308
  132.6 129.2 %copy-start.14 = (f32[256,1536]{1,0:T(8,128)}, f32[256,1536]{1,0:T(8,128)S(1)}, u32[]{:S(2)}) copy-start(f32[256,1536]{1,0:T(8,128)S(1)} %fusion.79) | copy-start | bytes 4718596
  132.7 30.7 %copy-start.50 = (s32[4,4]{1,0:T(4,128)S(1)}, s32[4,4]{1,0:T(4,128)}, u32[]{:S(2)}) copy-start(s32[4,4]{1,0:T(4,128)} %constant.240.clone.1) | copy-start | bytes 196
  132.7 30.7 %copy-start.51 = (s32[4,4]{1,0:T(4,128)S(1)}, s32[4,4]{1,0:T(4,128)}, u32[]{:S(2)}) copy-start(s32[4,4]{1,0:T(4,128)} %constant.241.clone.1) | copy-start | bytes 196
  132.7 30.9 %copy-start.52 = (bf16[512]{0:T(512)(128)(2,1)S(1)}, bf16[512]{0:T(512)(128)(2,1)}, u32[]{:S(2)}) copy-start(bf16[512]{0:T(512)(128)(2,1)} %param.32) | copy-start | bytes 3076
  132.9 124.8 %copy-start.22 = (f32[256,256]{0,1:T(8,128)}, f32[256,256]{0,1:T(8,128)S(1)}, u32[]{:S(2)}) copy-start(f32[256,256]{0,1:T(8,128)S(1)} %copy.182) | copy-start | bytes 786436
  133.0 30.5 %copy-start.39 = (f32[256,4]{0,1:T(4,128)}, f32[256,4]{0,1:T(4,128)S(1)}, u32[]{:S(2)}) copy-start(f32[256,4]{0,1:T(4,128)S(1)} %add_rsqrt_fusion.1) | copy-start | bytes 12292
  134.0 205.2 %all-gather.18.cloned.1.call-start = ((), (), s32[]{:S(2)}) async-start(), calls=%async_computation.8 | async-start | bytes 5242880 | tf_op jit(solution)/shard_map/all_gather | solution.py:107
  134.7 221.0 %all-gather.20.cloned.1.call-start = ((), (), s32[]{:S(2)}) async-start(), calls=%async_computation.9 | async-start | bytes 5242880 | tf_op jit(solution)/shard_map/all_gather | solution.py:112
  135.3 301.1 %all-gather.22.cloned.1.call-start = ((), (), s32[]{:S(2)}) async-start(), calls=%async_computation.10 | async-start | bytes 5242880 | tf_op jit(solution)/shard_map/all_gather | solution.py:113
  135.4 28.0 %collective-permute-start = (bf16[256,2048]{1,0:T(8,128)(2,1)S(1)}, bf16[256,2048]{1,0:T(8,128)(2,1)}, u32[]{:S(2)}, u32[]{:S(2)}) collective-permute-start(bf16[256,2048]{1,0:T(8,128)(2,1)S(1)} %copy-done.26), channel_id=1, source_target_pairs={{0,1},{1,2},{2,3},{3,0},{4,5},{5,6},{6,7},{7,4},{8,9},{9,10},{10,1... | collective-permute-start | bytes 3145736 | tf_op jit(solution)/shard_map/ppermute | solution.py:20
  135.4 123.8 %collective-permute-start.1 = (bf16[256,2048]{1,0:T(8,128)(2,1)S(1)}, bf16[256,2048]{1,0:T(8,128)(2,1)}, u32[]{:S(2)}, u32[]{:S(2)}) collective-permute-start(bf16[256,2048]{1,0:T(8,128)(2,1)S(1)} %copy-done.26), channel_id=1, source_target_pairs={{0,3},{1,0},{2,1},{3,2},{4,7},{5,4},{6,5},{7,6},{8,11},{9,8},{10,9... | collective-permute-start | bytes 3145736 | tf_op jit(solution)/shard_map/ppermute | solution.py:23
  139.3 443.3 %reduce-scatter.7.cloned.1.call-start = ((), (), s32[]{:S(2)}) async-start(), calls=%async_computation.11 | async-start | bytes 2359296 | tf_op jit(solution)/shard_map/reduce_scatter | solution.py:298
  163.4 97.2 %collective-permute-start.2 = (bf16[256,2048]{1,0:T(8,128)(2,1)}, bf16[256,2048]{1,0:T(8,128)(2,1)}, u32[]{:S(2)}, u32[]{:S(2)}) collective-permute-start(bf16[256,2048]{1,0:T(8,128)(2,1)} %collective-permute-done), channel_id=1, source_target_pairs={{0,1},{1,2},{2,3},{3,0},{4,5},{5,6},{6,7},{7,4},{8,9},{9,10},{10,1... | collective-permute-start | bytes 3145736 | tf_op jit(solution)/shard_map/ppermute | solution.py:20
  343.2 105.0 %copy-start.2 = (f32[256,2048]{1,0:T(8,128)}, f32[256,2048]{1,0:T(8,128)S(1)}, u32[]{:S(2)}) copy-start(f32[256,2048]{1,0:T(8,128)S(1)} %get-tuple-element.820) | copy-start | bytes 6291460
  436.4 4.3 copy-start.55
  443.3 5.0 copy-start.32
  452.7 22.7 %copy-start.1 = (f32[256,4,4,64]{0,3,2,1:T(8,128)S(1)}, f32[256,4,4,64]{0,3,2,1:T(8,128)}, u32[]{:S(2)}) copy-start(f32[256,4,4,64]{0,3,2,1:T(8,128)} %custom-call.4) | copy-start | bytes 3145732
  529.5 4.3 copy-start.13
  533.7 227.9 %reduce-scatter.11.cloned.1.call-start = ((), (), s32[]{:S(2)}) async-start(), calls=%async_computation.14 | async-start | bytes 8650752 | tf_op jit(solution)/shard_map/reduce_scatter | solution.py:348
  540.1 407.2 %reduce-scatter.13.cloned.1.call-start = ((), (), s32[]{:S(2)}) async-start(), calls=%async_computation.16 | async-start | bytes 8650752 | tf_op jit(solution)/shard_map/reduce_scatter | solution.py:349
  548.4 584.6 %reduce-scatter.15.cloned.1.call-start = ((), (), s32[]{:S(2)}) async-start(), calls=%async_computation.18 | async-start | bytes 8650752 | tf_op jit(solution)/shard_map/reduce_scatter | solution.py:350
  554.0 764.6 %reduce-scatter.17.cloned.1.call-start = ((), (), s32[]{:S(2)}) async-start(), calls=%async_computation.20 | async-start | bytes 8650752 | tf_op jit(solution)/shard_map/reduce_scatter | solution.py:351
  559.9 6.1 copy-start.36
  559.9 917.3 %reduce-scatter.9.cloned.1.call-start = ((), (), s32[]{:S(2)}) async-start(), calls=%async_computation.12 | async-start | bytes 12976128 | tf_op jit(solution)/shard_map/reduce_scatter | solution.py:347
  562.9 6.7 copy-start.40
  564.9 5.7 copy-start.28
  564.9 5.7 copy-start.30
  570.7 8.6 copy-start.15
  576.8 7.6 copy-start.23
  593.5 885.4 %copy-start.54 = (u32[32]{0:T(128)S(1)}, u32[32]{0:T(128)}, u32[]{:S(2)}) copy-start(u32[32]{0:T(128)} %constant.273) | copy-start | bytes 388
  593.5 887.5 %copy-start.41 = (f32[2048]{0:T(1024)S(1)}, f32[2048]{0:T(1024)}, u32[]{:S(2)}) copy-start(f32[2048]{0:T(1024)} %get-tuple-element.648) | copy-start | bytes 24580
  593.5 887.6 %copy-start.3 = (f32[256,2048]{1,0:T(8,128)S(1)}, f32[256,2048]{1,0:T(8,128)}, u32[]{:S(2)}) copy-start(f32[256,2048]{1,0:T(8,128)} %copy-done.2) | copy-start | bytes 6291460
  593.6 958.3 %all-gather.26.cloned.1.call-start = ((), (), s32[]{:S(2)}) async-start(), calls=%async_computation.15 | async-start | bytes 1179648 | tf_op jit(solution)/shard_map/all_gather | solution.py:360
  763.2 791.4 %all-gather.28.cloned.1.call-start = ((), (), s32[]{:S(2)}) async-start(), calls=%async_computation.17 | async-start | bytes 1179648 | tf_op jit(solution)/shard_map/all_gather | solution.py:363
  948.9 608.5 %all-gather.30.cloned.1.call-start = ((), (), s32[]{:S(2)}) async-start(), calls=%async_computation.19 | async-start | bytes 1179648 | tf_op jit(solution)/shard_map/all_gather | solution.py:366
  1134.7 443.2 %all-gather.32.cloned.1.call-start = ((), (), s32[]{:S(2)}) async-start(), calls=%async_computation.21 | async-start | bytes 1179648 | tf_op jit(solution)/shard_map/all_gather | solution.py:369
  1320.3 285.5 %all-gather.24.cloned.1.call-start = ((), (), s32[]{:S(2)}) async-start(), calls=%async_computation.13 | async-start | bytes 1769472 | tf_op jit(solution)/shard_map/all_gather | solution.py:357
  1478.9 7.3 copy-start.31
  1478.9 7.3 copy-start.43
  1486.2 62.1 %copy-start.5 = (f32[256,2048]{1,0:T(8,128)S(1)}, f32[256,2048]{1,0:T(8,128)}, u32[]{:S(2)}) copy-start(f32[256,2048]{1,0:T(8,128)} %copy-done.4) | copy-start | bytes 6291460
  (30 other events, 66.8 us)
Sparse Core Ops, SparseCore 0:
  9.6 118.0 all-gather.13
  134.1 25.9 all-gather.15
  161.7 111.7 all-gather.17
  274.9 80.7 all-gather.19
  357.1 79.2 all-gather.21
  533.8 39.6 reduce-scatter.6
  575.8 185.7 reduce-scatter.10
  763.9 183.3 reduce-scatter.12
  949.6 183.3 reduce-scatter.14
  1135.2 183.4 reduce-scatter.16
  1324.6 152.5 reduce-scatter.8
  1479.5 22.6 all-gather.25
  1504.1 23.3 all-gather.27
  1529.2 23.4 all-gather.29
  1554.4 23.3 all-gather.31
  1580.2 25.5 all-gather.23
